TPU v7x, 512 devices: a whole 4x8x8 slice. The times are simulated.
512 devices in a mesh: tile: 64 (over z, y), scan: 8 (over x, core).
Axes of the slice: x: 4, y: 8, z: 8, core: 2. Of those that a mesh axis runs over, the one named last changes fastest.
Arguments:
- object_real: float32 [3, 64, 128, 128], P(None, 'tile'), may hold values from 0.5 to 1.5
- object_imag: float32 [3, 64, 128, 128], P(None, 'tile'), may hold values from -1 to 1
- probe_modes: float32 [2, 2, 128, 128], replicated, may hold values from -6 to 6
- measured: float32 [64, 8, 1, 128, 128], P('tile', 'scan'), may hold values from 1 to 6
- offsets: int32 [64, 8, 1, 2], P('tile', 'scan'), may hold values from 0 to 127
- live: int32 [64, 8, 1], P('tile', 'scan'), may hold values 0 or 1
Outputs:
- object_real_out: float32 [3, 64, 128, 128], P(None, 'tile')
- object_imag_out: float32 [3, 64, 128, 128], P(None, 'tile')
- probe_out: float32 [2, 2, 128, 128], replicated
All inputs are finite; a program needn't handle non-finite values. No bound on the sum of `live` on one device may be relied on, other than what follows from the above.
Results may differ from a plain program's by a relative error of at most 0.0003.
Values sent between devices are 32-bit elements; how exact they have to be, the bound alone decides.
No kernel may reach another device: no remote copies, remote signals or barrier semaphores. Data moves between devices by JAX's collectives and lax.ppermute only.
A program may use at most 64 MiB of HBM per device.

v0:
```python
import math
import jax
import jax.numpy as jnp
from jax import lax
from jax.sharding import PartitionSpec as P

GRID = 8
ITERS = 2
object_rate = 0.008
probe_rate = 0.03


def shifted(shard, axis, by):
    size = lax.axis_size(axis)
    return lax.ppermute(shard, axis, [(i, (i + by) % size) for i in range(size)])


def make_tables(pattern_side):
    positions = lax.iota(jnp.int32, pattern_side)
    product = positions[:, None] * positions[None, :] % pattern_side
    angles = 2.0 * math.pi / pattern_side * product.astype(jnp.float32)
    scaling = 1.0 / math.sqrt(pattern_side)
    frequency = jnp.where(
        positions < pattern_side // 2, positions, positions - pattern_side
    ).astype(jnp.float32)
    phases = (
        -4.0
        * math.pi
        * (frequency[:, None] ** 2 + frequency[None, :] ** 2)
        / (pattern_side * pattern_side)
    )
    return (jnp.cos(angles) * scaling, jnp.sin(angles) * scaling, jnp.cos(phases), jnp.sin(phases))


def from_left(matrix, values):
    return jnp.einsum("jk,mkl->mjl", matrix, values, precision=lax.Precision.HIGHEST)


def from_right(values, matrix):
    return jnp.einsum("mjk,kl->mjl", values, matrix, precision=lax.Precision.HIGHEST)


def transform(part_real, part_imag, tables, sign):
    cosine, sine_table = (tables[0], tables[1])
    left_real = from_left(cosine, part_real) + sign * from_left(sine_table, part_imag)
    left_imag = from_left(cosine, part_imag) - sign * from_left(sine_table, part_real)
    out_real = from_right(left_real, cosine) + sign * from_right(left_imag, sine_table)
    out_imag = from_right(left_imag, cosine) - sign * from_right(left_real, sine_table)
    return (out_real, out_imag)


def slot_loss(patch_cells, mode_values, target, weight, tables):
    depth_count = patch_cells.shape[1]
    wave_real, wave_imag = (mode_values[:, 0], mode_values[:, 1])
    for depth_index in range(depth_count):
        cell_real = patch_cells[0, depth_index]
        cell_imag = patch_cells[1, depth_index]
        wave_real, wave_imag = (
            wave_real * cell_real - wave_imag * cell_imag,
            wave_real * cell_imag + wave_imag * cell_real,
        )
        if depth_index < depth_count - 1:
            freq_real, freq_imag = transform(wave_real, wave_imag, tables, 1.0)
            kern_real, kern_imag = (tables[2], tables[3])
            freq_real, freq_imag = (
                freq_real * kern_real - freq_imag * kern_imag,
                freq_real * kern_imag + freq_imag * kern_real,
            )
            wave_real, wave_imag = transform(freq_real, freq_imag, tables, -1.0)
    far_real, far_imag = transform(wave_real, wave_imag, tables, 1.0)
    intensity = jnp.sum(far_real**2 + far_imag**2, axis=0)
    return 0.5 * weight * jnp.sum((intensity - target) ** 2)


def local(object_real, object_imag, probe_modes, measured, offsets, live):
    slices = object_real.shape[0]
    block_side = object_real.shape[2]
    pattern_side = probe_modes.shape[2]
    slot_count = measured.shape[2]
    tile_count = lax.axis_size("tile")
    group_count = lax.axis_size("scan")
    tables = make_tables(pattern_side)
    anchor = jnp.zeros((), jnp.int32)
    obj_state = jnp.stack([object_real[:, 0], object_imag[:, 0]])
    for iteration in range(ITERS):
        right_part = shifted(obj_state, "tile", -1)
        below_part = shifted(obj_state, "tile", -GRID)
        corner_part = shifted(obj_state, "tile", -GRID - 1)
        upper_half = jnp.concatenate([obj_state, right_part], axis=-1)
        lower_half = jnp.concatenate([below_part, corner_part], axis=-1)
        canvas = jnp.concatenate([upper_half, lower_half], axis=-2)
        current_probe = probe_modes

        def visit_slot(slot_index, running):
            grad_canvas, grad_probe = running
            row_start = offsets[0, 0, slot_index, 0]
            col_start = offsets[0, 0, slot_index, 1]
            starts = (anchor, anchor, row_start, col_start)
            patch_cells = lax.dynamic_slice(canvas, starts, (2, slices, pattern_side, pattern_side))
            target = measured[0, 0, slot_index]
            weight = live[0, 0, slot_index].astype(jnp.float32)
            _, pullback = jax.vjp(
                lambda cell_values, mode_values: slot_loss(
                    cell_values, mode_values, target, weight, tables
                ),
                patch_cells,
                current_probe,
            )
            grad_patch, grad_modes = pullback(jnp.ones((), jnp.float32))
            current = lax.dynamic_slice(
                grad_canvas, starts, (2, slices, pattern_side, pattern_side)
            )
            grad_canvas = lax.dynamic_update_slice(grad_canvas, current + grad_patch, starts)
            return (grad_canvas, grad_probe + grad_modes)

        initial = (jnp.zeros_like(canvas), jnp.zeros_like(probe_modes))
        grad_canvas, grad_probe = lax.fori_loop(0, slot_count, visit_slot, initial)
        own_grad = grad_canvas[:, :, :block_side, :block_side]
        side_grad = grad_canvas[:, :, :block_side, block_side:]
        lower_grads = grad_canvas[:, :, block_side:, :]
        left_grad = shifted(side_grad, "tile", 1)
        above_grad = shifted(lower_grads[..., :block_side], "tile", GRID)
        diagonal_grad = shifted(lower_grads[..., block_side:], "tile", GRID + 1)
        grad_total = own_grad + above_grad + left_grad + diagonal_grad
        grad_total = lax.psum(grad_total, "scan")
        grad_probe = lax.psum(grad_probe, ("tile", "scan"))
        obj_state = obj_state - object_rate / (slot_count * group_count) * grad_total
        probe_modes = (
            probe_modes - probe_rate / (slot_count * tile_count * group_count) * grad_probe
        )
    return (obj_state[0][:, None], obj_state[1][:, None], probe_modes)


def solution(mesh):
    placed = (
        P(None, "tile", None, None),
        P(None, "tile", None, None),
        P(),
        P("tile", "scan", None, None, None),
        P("tile", "scan", None, None),
        P("tile", "scan", None),
    )
    return jax.shard_map(
        local,
        mesh=mesh,
        in_specs=placed,
        out_specs=(P(None, "tile", None, None), P(None, "tile", None, None), P()),
        check_vma=False,
    )
```

profile of v0, /device:TPU:8, one launch (start us, length us, event | category | flops | bytes accessed | tf_op | source)
XLA Modules:
  0.0 896.9 jit_solution(5106531731478892876)
XLA Ops:
  8.1 1.1 pad_maximum_fusion
  9.2 10.9 %collective-permute-start.1 = (f32[2,3,128,128]{3,2,1,0:T(8,128)S(1)}, f32[2,3,128,128]{3,2,1,0:T(8,128)S(1)}, u32[]{:S(2)}, u32[]{:S(2)}) collective-permute-start(f32[2,3,128,128]{3,2,1,0:T(8,128)S(1)} %pad_maximum_fusion), channel_id=1, source_target_pairs={{0,448},{8,456},{16,464},{24,472},{32,480},{40,488},{48,496},{56,5... | collective-permute-start | bytes 1179656 | tf_op jit(solution)/shard_map/ppermute | solution.py:15
  20.2 2.3 collective-permute-start.2
  22.5 5.4 collective-permute-start
  27.9 1.3 fusion.1195
  32.4 1.1 copy.315
  35.2 1.8 collective-permute-done.1
  36.9 4.1 collective-permute-done
  46.2 0.6 convolution_multiply_fusion.14
  46.7 0.6 convolution_multiply_fusion.15
  51.8 0.6 fusion.54
  53.0 0.6 fusion.55
  53.6 0.9 fusion.330
  55.6 0.6 convolution_multiply_fusion.10
  56.2 0.6 convolution_multiply_fusion.11
  61.3 0.6 fusion.50
  62.4 0.6 fusion.51
  66.8 0.7 fusion.311
  80.7 0.7 fusion.36
  86.4 0.6 add_bitcast_fusion.3
  87.6 4.1 dynamic_update_slice.8
  91.8 3.3 collective-permute-start.3
  95.2 3.2 collective-permute-start.5
  98.3 4.5 collective-permute-start.4
  102.8 2.2 collective-permute-done.3
  105.0 13.5 %collective-permute-done.5 = f32[2,3,128,128]{3,2,1,0:T(8,128)S(1)} collective-permute-done((f32[2,3,128,128]{3,2,1,0:T(8,128)S(1)}, f32[2,3,128,128]{3,2,1,0:T(8,128)S(1)}, u32[]{:S(2)}, u32[]{:S(2)}) %collective-permute-start.5) | collective-permute-done | bytes 393248 | tf_op jit(solution)/shard_map/ppermute | solution.py:15
  118.5 4.8 collective-permute-done.4
  123.3 0.8 fusion.70
  124.2 80.1 %all-reduce.21.cloned.1.call-done = f32[2,3,128,128]{3,2,1,0:T(8,128)} async-done(((f32[2,3,128,128]{3,2,1,0:T(8,128)}), f32[2,3,128,128]{3,2,1,0:T(8,128)}) %all-reduce.21.cloned.1.call-update) | async-done | bytes 393232 | tf_op jit(solution)/shard_map/psum | solution.py:125
  204.3 1.0 multiply_subtract_fusion.1
  205.4 5.8 collective-permute-start.8
  211.2 3.2 collective-permute-start.7
  214.4 5.5 collective-permute-start.6
  219.9 0.7 pad_add_fusion.3
  221.1 262.6 %all-reduce.23.cloned.1.call-done = f32[2,2,128,128]{2,3,0,1:T(8,128)} async-done(((f32[2,2,128,128]{2,3,0,1:T(8,128)}), f32[2,2,128,128]{2,3,0,1:T(8,128)}) %all-reduce.23.cloned.1.call-update) | async-done | bytes 262160 | tf_op jit(solution)/shard_map/psum | solution.py:126
  483.7 1.0 multiply_subtract_fusion.3
  489.8 0.6 convolution_multiply_fusion.6
  490.4 0.6 convolution_multiply_fusion.7
  495.5 0.6 fusion.24
  496.6 0.6 fusion.25
  497.7 0.7 convolution_subtract_fusion.4
  499.0 0.6 convolution_multiply_fusion.2
  499.6 0.6 convolution_multiply_fusion.3
  501.3 0.6 fusion.23
  504.7 0.6 fusion.20
  505.8 0.6 fusion.21
  510.8 0.7 fusion.18
  524.7 0.8 fusion.4
  529.9 0.6 add_bitcast_fusion.1
  531.1 4.1 dynamic_update_slice.9
  535.2 1.0 fusion.1193
  536.3 3.5 collective-permute-start.9
  539.8 3.4 collective-permute-start.11
  543.2 2.8 collective-permute-start.10
  546.0 0.7 pad_add_fusion.2
  546.8 12.8 %collective-permute-done.9 = f32[2,3,128,128]{3,2,1,0:T(8,128)} collective-permute-done((f32[2,3,128,128]{3,2,1,0:T(8,128)}, f32[2,3,128,128]{3,2,1,0:T(8,128)}, u32[]{:S(2)}, u32[]{:S(2)}) %collective-permute-start.9) | collective-permute-done | bytes 393248 | tf_op jit(solution)/shard_map/ppermute | solution.py:15
  559.7 1.4 collective-permute-done.10
  561.1 2.1 fusion.68
  563.2 253.8 %all-reduce.27.cloned.1.call-done = f32[2,2,128,128]{2,3,0,1:T(8,128)} async-done(((f32[2,2,128,128]{2,3,0,1:T(8,128)}), f32[2,2,128,128]{2,3,0,1:T(8,128)}) %all-reduce.27.cloned.1.call-update) | async-done | bytes 262160 | tf_op jit(solution)/shard_map/psum | solution.py:126
  817.0 1.0 multiply_subtract_fusion.2
  818.0 0.8 copy.474
  818.8 68.3 %all-reduce.25.cloned.1.call-done = f32[2,3,128,128]{3,2,1,0:T(8,128)} async-done(((f32[2,3,128,128]{3,2,1,0:T(8,128)}), f32[2,3,128,128]{3,2,1,0:T(8,128)}) %all-reduce.25.cloned.1.call-update) | async-done | bytes 393232 | tf_op jit(solution)/shard_map/psum | solution.py:125
  887.1 1.1 multiply_subtract_fusion
  888.1 0.8 slice_bitcast_fusion
  (190 shorter events, 77.2 us)
Async XLA Ops:
  8.0 33.1 %copy-start.1 = (f32[3,1,128,128]{3,2,1,0:T(8,128)S(1)}, f32[3,1,128,128]{3,2,1,0:T(8,128)}, u32[]{:S(2)}) copy-start(f32[3,1,128,128]{3,2,1,0:T(8,128)} %param.7) | copy-start | bytes 589828
  8.0 33.1 %copy-start = (f32[3,1,128,128]{3,2,1,0:T(8,128)S(1)}, f32[3,1,128,128]{3,2,1,0:T(8,128)}, u32[]{:S(2)}) copy-start(f32[3,1,128,128]{3,2,1,0:T(8,128)} %param.6) | copy-start | bytes 589828
  8.0 196.3 %all-reduce.21.cloned.1.call-start = ((), (), s32[]{:S(2)}) async-start(), calls=%async_computation | async-start | bytes 786432 | tf_op jit(solution)/shard_map/psum | solution.py:125
  9.2 27.7 %collective-permute-start.1 = (f32[2,3,128,128]{3,2,1,0:T(8,128)S(1)}, f32[2,3,128,128]{3,2,1,0:T(8,128)S(1)}, u32[]{:S(2)}, u32[]{:S(2)}) collective-permute-start(f32[2,3,128,128]{3,2,1,0:T(8,128)S(1)} %pad_maximum_fusion), channel_id=1, source_target_pairs={{0,448},{8,456},{16,464},{24,472},{32,480},{40,488},{48,496},{56,5... | collective-permute-start | bytes 1179656 | tf_op jit(solution)/shard_map/ppermute | solution.py:15
  20.2 16.8 %collective-permute-start.2 = (f32[2,3,128,128]{3,2,1,0:T(8,128)S(1)}, f32[2,3,128,128]{3,2,1,0:T(8,128)S(1)}, u32[]{:S(2)}, u32[]{:S(2)}) collective-permute-start(f32[2,3,128,128]{3,2,1,0:T(8,128)S(1)} %pad_maximum_fusion), channel_id=1, source_target_pairs={{0,440},{8,448},{16,456},{24,464},{32,472},{40,480},{48,488},{56,4... | collective-permute-start | bytes 1179656 | tf_op jit(solution)/shard_map/ppermute | solution.py:15
  22.5 18.6 %collective-permute-start = (f32[2,3,128,128]{3,2,1,0:T(8,128)S(1)}, f32[2,3,128,128]{3,2,1,0:T(8,128)S(1)}, u32[]{:S(2)}, u32[]{:S(2)}) collective-permute-start(f32[2,3,128,128]{3,2,1,0:T(8,128)S(1)} %pad_maximum_fusion), channel_id=1, source_target_pairs={{0,504},{8,0},{16,8},{24,16},{32,24},{40,32},{48,40},{56,48},{64,5... | collective-permute-start | bytes 1179656 | tf_op jit(solution)/shard_map/ppermute | solution.py:15
  60.7 4.0 copy-start.3
  91.8 13.2 %collective-permute-start.3 = (f32[2,3,128,128]{3,2,1,0:T(8,128)S(1)}, f32[2,3,128,128]{3,2,1,0:T(8,128)S(1)}, u32[]{:S(2)}, u32[]{:S(2)}) collective-permute-start(f32[2,3,128,128]{3,2,1,0:T(8,128)S(1)} %get-tuple-element.121), channel_id=1, source_target_pairs={{0,64},{8,72},{16,80},{24,88},{32,96},{40,104},{48,112},{56,120},{... | collective-permute-start | bytes 1179656 | tf_op jit(solution)/shard_map/ppermute | solution.py:15
  95.2 23.4 %collective-permute-start.5 = (f32[2,3,128,128]{3,2,1,0:T(8,128)S(1)}, f32[2,3,128,128]{3,2,1,0:T(8,128)S(1)}, u32[]{:S(2)}, u32[]{:S(2)}) collective-permute-start(f32[2,3,128,128]{3,2,1,0:T(8,128)S(1)} %get-tuple-element.122), channel_id=1, source_target_pairs={{0,72},{8,80},{16,88},{24,96},{32,104},{40,112},{48,120},{56,128},... | collective-permute-start | bytes 1179656 | tf_op jit(solution)/shard_map/ppermute | solution.py:15
  98.3 25.0 %collective-permute-start.4 = (f32[2,3,128,128]{3,2,1,0:T(8,128)S(1)}, f32[2,3,128,128]{3,2,1,0:T(8,128)S(1)}, u32[]{:S(2)}, u32[]{:S(2)}) collective-permute-start(f32[2,3,128,128]{3,2,1,0:T(8,128)S(1)} %get-tuple-element.123), channel_id=1, source_target_pairs={{0,8},{8,16},{16,24},{24,32},{32,40},{40,48},{48,56},{56,64},{64,7... | collective-permute-start | bytes 1179656 | tf_op jit(solution)/shard_map/ppermute | solution.py:15
  124.2 359.5 %all-reduce.23.cloned.1.call-start = ((), (), s32[]{:S(2)}) async-start(), calls=%async_computation.1 | async-start | bytes 524288 | tf_op jit(solution)/shard_map/psum | solution.py:126
  205.4 279.3 %collective-permute-start.8 = (f32[2,3,128,128]{3,2,1,0:T(8,128)S(1)}, f32[2,3,128,128]{3,2,1,0:T(8,128)S(1)}, u32[]{:S(2)}, u32[]{:S(2)}) collective-permute-start(f32[2,3,128,128]{3,2,1,0:T(8,128)S(1)} %multiply_subtract_fusion.1), channel_id=1, source_target_pairs={{0,440},{8,448},{16,456},{24,464},{32,472},{40,480},{48,488},{56,4... | collective-permute-start | bytes 1179656 | tf_op jit(solution)/shard_map/ppermute | solution.py:15
  211.2 273.5 %collective-permute-start.7 = (f32[2,3,128,128]{3,2,1,0:T(8,128)S(1)}, f32[2,3,128,128]{3,2,1,0:T(8,128)S(1)}, u32[]{:S(2)}, u32[]{:S(2)}) collective-permute-start(f32[2,3,128,128]{3,2,1,0:T(8,128)S(1)} %multiply_subtract_fusion.1), channel_id=1, source_target_pairs={{0,448},{8,456},{16,464},{24,472},{32,480},{40,488},{48,496},{56,5... | collective-permute-start | bytes 1179656 | tf_op jit(solution)/shard_map/ppermute | solution.py:15
  214.4 270.3 %collective-permute-start.6 = (f32[2,3,128,128]{3,2,1,0:T(8,128)S(1)}, f32[2,3,128,128]{3,2,1,0:T(8,128)S(1)}, u32[]{:S(2)}, u32[]{:S(2)}) collective-permute-start(f32[2,3,128,128]{3,2,1,0:T(8,128)S(1)} %multiply_subtract_fusion.1), channel_id=1, source_target_pairs={{0,504},{8,0},{16,8},{24,16},{32,24},{40,32},{48,40},{56,48},{64,5... | collective-permute-start | bytes 1179656 | tf_op jit(solution)/shard_map/ppermute | solution.py:15
  220.6 596.3 %all-reduce.27.cloned.1.call-start = ((), (), s32[]{:S(2)}) async-start(), calls=%async_computation.3 | async-start | bytes 524288 | tf_op jit(solution)/shard_map/psum | solution.py:126
  536.3 23.4 %collective-permute-start.9 = (f32[2,3,128,128]{3,2,1,0:T(8,128)}, f32[2,3,128,128]{3,2,1,0:T(8,128)}, u32[]{:S(2)}, u32[]{:S(2)}) collective-permute-start(f32[2,3,128,128]{3,2,1,0:T(8,128)} %get-tuple-element.118), channel_id=1, source_target_pairs={{0,64},{8,72},{16,80},{24,88},{32,96},{40,104},{48,112},{56,120},{... | collective-permute-start | bytes 1179656 | tf_op jit(solution)/shard_map/ppermute | solution.py:15
  539.8 19.9 %collective-permute-start.11 = (f32[2,3,128,128]{3,2,1,0:T(8,128)}, f32[2,3,128,128]{3,2,1,0:T(8,128)}, u32[]{:S(2)}, u32[]{:S(2)}) collective-permute-start(f32[2,3,128,128]{3,2,1,0:T(8,128)} %get-tuple-element.119), channel_id=1, source_target_pairs={{0,72},{8,80},{16,88},{24,96},{32,104},{40,112},{48,120},{56,128},... | collective-permute-start | bytes 1179656 | tf_op jit(solution)/shard_map/ppermute | solution.py:15
  543.2 17.9 %collective-permute-start.10 = (f32[2,3,128,128]{3,2,1,0:T(8,128)S(1)}, f32[2,3,128,128]{3,2,1,0:T(8,128)}, u32[]{:S(2)}, u32[]{:S(2)}) collective-permute-start(f32[2,3,128,128]{3,2,1,0:T(8,128)S(1)} %get-tuple-element.120), channel_id=1, source_target_pairs={{0,8},{8,16},{16,24},{24,32},{32,40},{40,48},{48,56},{56,64},{64,7... | collective-permute-start | bytes 1179656 | tf_op jit(solution)/shard_map/ppermute | solution.py:15
  546.8 340.3 %copy-start.2 = (f32[2,3,128,128]{3,2,1,0:T(8,128)S(1)}, f32[2,3,128,128]{3,2,1,0:T(8,128)}, u32[]{:S(2)}) copy-start(f32[2,3,128,128]{3,2,1,0:T(8,128)} %all-reduce.21.cloned.1.call-done) | copy-start | bytes 1179652
  546.8 340.3 %all-reduce.25.cloned.1.call-start = ((), (), s32[]{:S(2)}) async-start(), calls=%async_computation.2 | async-start | bytes 786432 | tf_op jit(solution)/shard_map/psum | solution.py:125
Sparse Core Ops, SparseCore 0:
  124.3 79.9 all-reduce.20
Sparse Core Ops, SparseCore 1:
  220.7 262.9 all-reduce.22
  546.8 270.1 all-reduce.26
  819.3 67.7 all-reduce.24
where the time goes:
time: 906 us; the launch traced here: 897 us
  waiting for transfers between devices  706 us (78%)
  matrix products  88.9 us (10%)
  starting transfers between devices  54.4 us (6%)
  between operations  22.3 us (2%)
  local copies, waits for them, and re-layouts  14.7 us (2%)
  other arithmetic  11 us (1%)
    psum x2, waiting for transfers between devices, local(): grad_probe = lax.psum(grad_probe, ('tile', 'scan'))  516 us
    psum x2, waiting for transfers between devices, local(): grad_total = lax.psum(grad_total, 'scan')  148 us
    ppermute x12, starting transfers between devices, shifted(): lax.ppermute(shard, axis, [(i, (i + by) % size) for i in range(size)])  53.8 us
    dot_general x80, matrix products, from_left(): jnp.einsum('jk,mkl->mjl', matrix, values, precision=lax.Precision.HIGHEST)  44.9 us
    dot_general x80, matrix products, from_right(): jnp.einsum('mjk,kl->mjl', values, matrix, precision=lax.Precision.HIGHEST)  44 us
    ppermute x12, waiting for transfers between devices, shifted(): lax.ppermute(shard, axis, [(i, (i + by) % size) for i in range(size)])  40.7 us
  transfers between devices with their start and end apart: 16, of which 11 were waited for; matrix products, arithmetic and copies ran while one was open for 1% of the time, Pallas kernels for 0%

commit v1 on v0

--- a/solution.py
+++ b/solution.py
@@ -123,7 +123,7 @@
         diagonal_grad = shifted(lower_grads[..., block_side:], "tile", GRID + 1)
         grad_total = own_grad + above_grad + left_grad + diagonal_grad
         grad_total = lax.psum(grad_total, "scan")
-        grad_probe = lax.psum(grad_probe, ("tile", "scan"))
+        grad_probe = lax.psum(lax.psum(grad_probe, "tile"), "scan")
         obj_state = obj_state - object_rate / (slot_count * group_count) * grad_total
         probe_modes = (
             probe_modes - probe_rate / (slot_count * tile_count * group_count) * grad_probe

time: 906 us -> 685 us (0.76)
  waiting for transfers between devices: 706 us -> 485 us
    psum x2, waiting for transfers between devices: 516 us -> 291 us  [local(): grad_probe = lax.psum(lax.psum(grad_probe, 'tile'), 'scan')]
    ppermute x12, waiting for transfers between devices: 40.7 us -> 50.6 us  [shifted(): lax.ppermute(shard, axis, [(i, (i + by) % size) for i in range(size)])]
  transfers between devices with their start and end apart: 16 -> 16, of which waited for: 11 -> 14; matrix products, arithmetic and copies ran while one was open for 1% -> 1% of each run, Pallas kernels for 0% -> 0%
where the time goes in v1:
time: 685 us; the launch traced here: 676 us
  waiting for transfers between devices  485 us (71%)
  matrix products  89 us (13%)
  starting transfers between devices  54.8 us (8%)
  between operations  20.4 us (3%)
  local copies, waits for them, and re-layouts  15.5 us (2%)
  other arithmetic  11.4 us (2%)
    psum x2, waiting for transfers between devices, local(): grad_probe = lax.psum(lax.psum(grad_probe, 'tile'), 'scan')  291 us
    psum x2, waiting for transfers between devices, local(): grad_total = lax.psum(grad_total, 'scan')  143 us
    ppermute x12, starting transfers between devices, shifted(): lax.ppermute(shard, axis, [(i, (i + by) % size) for i in range(size)])  54.6 us
    ppermute x12, waiting for transfers between devices, shifted(): lax.ppermute(shard, axis, [(i, (i + by) % size) for i in range(size)])  50.6 us
    dot_general x80, matrix products, from_left(): jnp.einsum('jk,mkl->mjl', matrix, values, precision=lax.Precision.HIGHEST)  44.9 us
    dot_general x80, matrix products, from_right(): jnp.einsum('mjk,kl->mjl', values, matrix, precision=lax.Precision.HIGHEST)  44.1 us
  transfers between devices with their start and end apart: 16, of which 14 were waited for; matrix products, arithmetic and copies ran while one was open for 1% of the time, Pallas kernels for 0%

profile of v1, /device:TPU:8, one launch (start us, length us, event | category | flops | bytes accessed | tf_op | source)
XLA Modules:
  0.0 675.8 jit_solution(17537170591981041838)
XLA Ops:
  7.2 1.1 pad_maximum_fusion
  8.4 10.9 %collective-permute-start.1 = (f32[2,3,128,128]{3,2,1,0:T(8,128)S(1)}, f32[2,3,128,128]{3,2,1,0:T(8,128)S(1)}, u32[]{:S(2)}, u32[]{:S(2)}) collective-permute-start(f32[2,3,128,128]{3,2,1,0:T(8,128)S(1)} %pad_maximum_fusion), channel_id=1, source_target_pairs={{0,448},{8,456},{16,464},{24,472},{32,480},{40,488},{48,496},{56,5... | collective-permute-start | bytes 1179656 | tf_op jit(solution)/shard_map/ppermute | solution.py:15
  19.3 2.3 collective-permute-start.2
  21.7 5.4 collective-permute-start
  27.1 1.3 fusion.1195
  31.6 1.1 copy.315
  34.3 1.8 collective-permute-done.1
  36.1 4.1 collective-permute-done
  45.3 0.6 convolution_multiply_fusion.14
  45.9 0.6 convolution_multiply_fusion.15
  51.0 0.6 fusion.54
  52.2 0.6 fusion.55
  52.7 0.9 fusion.330
  55.3 0.6 convolution_multiply_fusion.11
  60.5 0.6 fusion.50
  61.6 0.6 fusion.51
  66.0 0.7 fusion.311
  79.9 0.7 fusion.36
  85.6 0.6 add_bitcast_fusion.3
  86.8 4.1 dynamic_update_slice.8
  90.9 0.9 fusion.1194
  91.8 3.3 collective-permute-start.3
  95.1 3.2 collective-permute-start.5
  98.3 4.5 collective-permute-start.4
  102.8 0.7 pad_add_fusion.3
  103.6 1.7 collective-permute-done.3
  105.3 13.3 %collective-permute-done.5 = f32[2,3,128,128]{3,2,1,0:T(8,128)} collective-permute-done((f32[2,3,128,128]{3,2,1,0:T(8,128)S(1)}, f32[2,3,128,128]{3,2,1,0:T(8,128)}, u32[]{:S(2)}, u32[]{:S(2)}) %collective-permute-start.5) | collective-permute-done | bytes 393248 | tf_op jit(solution)/shard_map/ppermute | solution.py:15
  118.6 4.8 collective-permute-done.4
  123.4 2.1 fusion.70
  125.4 141.1 %all-reduce.23.cloned.1.call-done = f32[2,2,128,128]{2,3,0,1:T(8,128)} async-done(((f32[2,2,128,128]{2,3,0,1:T(8,128)}), f32[2,2,128,128]{2,3,0,1:T(8,128)}) %all-reduce.23.cloned.1.call-update) | async-done | bytes 262160 | tf_op jit(solution)/shard_map/psum | solution.py:126
  266.6 71.6 %all-reduce.29.cloned.1.call-done = (f32[2,3,128,128]{3,2,1,0:T(8,128)}, f32[2,2,128,128]{2,3,0,1:T(8,128)}) async-done(((f32[2,3,128,128]{3,2,1,0:T(8,128)}, f32[2,2,128,128]{2,3,0,1:T(8,128)}), (f32[2,3,128,128]{3,2,1,0:T(8,128)}, f32[2,2,128,128]{2,3,0,1:T(8,128)})) %all-reduce.29.cloned.1.call-update) | async-done | bytes 655376 | tf_op jit(solution)/shard_map/psum | solution.py:125
  338.2 1.0 multiply_subtract_fusion.1
  339.3 5.8 collective-permute-start.8
  345.1 3.2 collective-permute-start.7
  348.3 5.9 collective-permute-start.6
  354.2 1.0 multiply_subtract_fusion.3
  355.2 5.6 collective-permute-done.7
  360.8 1.1 collective-permute-done.6
  366.9 0.6 convolution_multiply_fusion.6
  372.6 0.6 fusion.24
  373.7 0.6 fusion.25
  374.9 0.7 convolution_subtract_fusion.4
  376.2 0.6 convolution_multiply_fusion.2
  376.7 0.6 convolution_multiply_fusion.3
  381.8 0.6 fusion.20
  383.0 0.6 fusion.21
  388.0 0.7 fusion.18
  401.9 0.8 fusion.4
  407.0 0.6 add_bitcast_fusion.1
  408.3 4.1 dynamic_update_slice.9
  412.4 1.0 fusion.1193
  413.4 1.9 collective-permute-start.9
  415.3 3.8 collective-permute-start.11
  419.1 4.5 collective-permute-start.10
  423.6 0.7 pad_add_fusion.2
  424.4 3.3 collective-permute-done.9
  427.7 12.9 %collective-permute-done.11 = f32[2,3,128,128]{3,2,1,0:T(8,128)} collective-permute-done((f32[2,3,128,128]{3,2,1,0:T(8,128)}, f32[2,3,128,128]{3,2,1,0:T(8,128)}, u32[]{:S(2)}, u32[]{:S(2)}) %collective-permute-start.11) | collective-permute-done | bytes 393248 | tf_op jit(solution)/shard_map/ppermute | solution.py:15
  440.6 2.0 collective-permute-done.10
  442.6 2.0 fusion.68
  444.6 150.0 %all-reduce.25.cloned.1.call-done = f32[2,2,128,128]{2,3,0,1:T(8,128)} async-done(((f32[2,2,128,128]{2,3,0,1:T(8,128)}), f32[2,2,128,128]{2,3,0,1:T(8,128)}) %all-reduce.25.cloned.1.call-update) | async-done | bytes 262160 | tf_op jit(solution)/shard_map/psum | solution.py:126
  594.6 71.4 %all-reduce.27.cloned.1.call-done = (f32[2,3,128,128]{3,2,1,0:T(8,128)}, f32[2,2,128,128]{2,3,0,1:T(8,128)}) async-done(((f32[2,3,128,128]{3,2,1,0:T(8,128)}, f32[2,2,128,128]{2,3,0,1:T(8,128)}), (f32[2,3,128,128]{3,2,1,0:T(8,128)}, f32[2,2,128,128]{2,3,0,1:T(8,128)})) %all-reduce.27.cloned.1.call-update) | async-done | bytes 655376 | tf_op jit(solution)/shard_map/psum | solution.py:125
  666.0 1.1 multiply_subtract_fusion
  667.2 0.8 copy.474
  668.0 0.8 slice_bitcast_fusion
  (192 shorter events, 78.5 us)
Async XLA Ops:
  7.2 33.1 %copy-start.1 = (f32[3,1,128,128]{3,2,1,0:T(8,128)S(1)}, f32[3,1,128,128]{3,2,1,0:T(8,128)}, u32[]{:S(2)}) copy-start(f32[3,1,128,128]{3,2,1,0:T(8,128)} %param.7) | copy-start | bytes 589828
  7.2 33.1 %copy-start = (f32[3,1,128,128]{3,2,1,0:T(8,128)S(1)}, f32[3,1,128,128]{3,2,1,0:T(8,128)}, u32[]{:S(2)}) copy-start(f32[3,1,128,128]{3,2,1,0:T(8,128)} %param.6) | copy-start | bytes 589828
  7.2 259.4 %all-reduce.23.cloned.1.call-start = ((), (), s32[]{:S(2)}) async-start(), calls=%async_computation | async-start | bytes 524288 | tf_op jit(solution)/shard_map/psum | solution.py:126
  8.4 27.7 %collective-permute-start.1 = (f32[2,3,128,128]{3,2,1,0:T(8,128)S(1)}, f32[2,3,128,128]{3,2,1,0:T(8,128)S(1)}, u32[]{:S(2)}, u32[]{:S(2)}) collective-permute-start(f32[2,3,128,128]{3,2,1,0:T(8,128)S(1)} %pad_maximum_fusion), channel_id=1, source_target_pairs={{0,448},{8,456},{16,464},{24,472},{32,480},{40,488},{48,496},{56,5... | collective-permute-start | bytes 1179656 | tf_op jit(solution)/shard_map/ppermute | solution.py:15
  19.3 16.8 %collective-permute-start.2 = (f32[2,3,128,128]{3,2,1,0:T(8,128)S(1)}, f32[2,3,128,128]{3,2,1,0:T(8,128)S(1)}, u32[]{:S(2)}, u32[]{:S(2)}) collective-permute-start(f32[2,3,128,128]{3,2,1,0:T(8,128)S(1)} %pad_maximum_fusion), channel_id=1, source_target_pairs={{0,440},{8,448},{16,456},{24,464},{32,472},{40,480},{48,488},{56,4... | collective-permute-start | bytes 1179656 | tf_op jit(solution)/shard_map/ppermute | solution.py:15
  21.7 18.6 %collective-permute-start = (f32[2,3,128,128]{3,2,1,0:T(8,128)S(1)}, f32[2,3,128,128]{3,2,1,0:T(8,128)S(1)}, u32[]{:S(2)}, u32[]{:S(2)}) collective-permute-start(f32[2,3,128,128]{3,2,1,0:T(8,128)S(1)} %pad_maximum_fusion), channel_id=1, source_target_pairs={{0,504},{8,0},{16,8},{24,16},{32,24},{40,32},{48,40},{56,48},{64,5... | collective-permute-start | bytes 1179656 | tf_op jit(solution)/shard_map/ppermute | solution.py:15
  59.9 4.0 copy-start.4
  91.8 13.5 %collective-permute-start.3 = (f32[2,3,128,128]{3,2,1,0:T(8,128)}, f32[2,3,128,128]{3,2,1,0:T(8,128)}, u32[]{:S(2)}, u32[]{:S(2)}) collective-permute-start(f32[2,3,128,128]{3,2,1,0:T(8,128)} %get-tuple-element.125), channel_id=1, source_target_pairs={{0,64},{8,72},{16,80},{24,88},{32,96},{40,104},{48,112},{56,120},{... | collective-permute-start | bytes 1179656 | tf_op jit(solution)/shard_map/ppermute | solution.py:15
  95.1 23.5 %collective-permute-start.5 = (f32[2,3,128,128]{3,2,1,0:T(8,128)S(1)}, f32[2,3,128,128]{3,2,1,0:T(8,128)}, u32[]{:S(2)}, u32[]{:S(2)}) collective-permute-start(f32[2,3,128,128]{3,2,1,0:T(8,128)S(1)} %get-tuple-element.126), channel_id=1, source_target_pairs={{0,72},{8,80},{16,88},{24,96},{32,104},{40,112},{48,120},{56,128},... | collective-permute-start | bytes 1179656 | tf_op jit(solution)/shard_map/ppermute | solution.py:15
  98.3 25.1 %collective-permute-start.4 = (f32[2,3,128,128]{3,2,1,0:T(8,128)S(1)}, f32[2,3,128,128]{3,2,1,0:T(8,128)}, u32[]{:S(2)}, u32[]{:S(2)}) collective-permute-start(f32[2,3,128,128]{3,2,1,0:T(8,128)S(1)} %get-tuple-element.127), channel_id=1, source_target_pairs={{0,8},{8,16},{16,24},{24,32},{32,40},{40,48},{48,56},{56,64},{64,7... | collective-permute-start | bytes 1179656 | tf_op jit(solution)/shard_map/ppermute | solution.py:15
  103.5 234.7 %all-reduce.29.cloned.1.call-start = ((), (), s32[]{:S(2)}) async-start(), calls=%async_computation.3 | async-start | bytes 1310720 | tf_op jit(solution)/shard_map/psum | solution.py:125
  266.6 328.0 %all-reduce.25.cloned.1.call-start = ((), (), s32[]{:S(2)}) async-start(), calls=%async_computation.1 | async-start | bytes 524288 | tf_op jit(solution)/shard_map/psum | solution.py:126
  339.3 15.9 %collective-permute-start.8 = (f32[2,3,128,128]{3,2,1,0:T(8,128)S(1)}, f32[2,3,128,128]{3,2,1,0:T(8,128)S(1)}, u32[]{:S(2)}, u32[]{:S(2)}) collective-permute-start(f32[2,3,128,128]{3,2,1,0:T(8,128)S(1)} %multiply_subtract_fusion.1), channel_id=1, source_target_pairs={{0,440},{8,448},{16,456},{24,464},{32,472},{40,480},{48,488},{56,4... | collective-permute-start | bytes 1179656 | tf_op jit(solution)/shard_map/ppermute | solution.py:15
  345.1 15.6 %collective-permute-start.7 = (f32[2,3,128,128]{3,2,1,0:T(8,128)S(1)}, f32[2,3,128,128]{3,2,1,0:T(8,128)S(1)}, u32[]{:S(2)}, u32[]{:S(2)}) collective-permute-start(f32[2,3,128,128]{3,2,1,0:T(8,128)S(1)} %multiply_subtract_fusion.1), channel_id=1, source_target_pairs={{0,448},{8,456},{16,464},{24,472},{32,480},{40,488},{48,496},{56,5... | collective-permute-start | bytes 1179656 | tf_op jit(solution)/shard_map/ppermute | solution.py:15
  348.3 13.5 %collective-permute-start.6 = (f32[2,3,128,128]{3,2,1,0:T(8,128)S(1)}, f32[2,3,128,128]{3,2,1,0:T(8,128)S(1)}, u32[]{:S(2)}, u32[]{:S(2)}) collective-permute-start(f32[2,3,128,128]{3,2,1,0:T(8,128)S(1)} %multiply_subtract_fusion.1), channel_id=1, source_target_pairs={{0,504},{8,0},{16,8},{24,16},{32,24},{40,32},{48,40},{56,48},{64,5... | collective-permute-start | bytes 1179656 | tf_op jit(solution)/shard_map/ppermute | solution.py:15
  413.4 14.3 %collective-permute-start.9 = (f32[2,3,128,128]{3,2,1,0:T(8,128)}, f32[2,3,128,128]{3,2,1,0:T(8,128)}, u32[]{:S(2)}, u32[]{:S(2)}) collective-permute-start(f32[2,3,128,128]{3,2,1,0:T(8,128)} %get-tuple-element.122), channel_id=1, source_target_pairs={{0,64},{8,72},{16,80},{24,88},{32,96},{40,104},{48,112},{56,120},{... | collective-permute-start | bytes 1179656 | tf_op jit(solution)/shard_map/ppermute | solution.py:15
  415.3 25.2 %collective-permute-start.11 = (f32[2,3,128,128]{3,2,1,0:T(8,128)}, f32[2,3,128,128]{3,2,1,0:T(8,128)}, u32[]{:S(2)}, u32[]{:S(2)}) collective-permute-start(f32[2,3,128,128]{3,2,1,0:T(8,128)} %get-tuple-element.123), channel_id=1, source_target_pairs={{0,72},{8,80},{16,88},{24,96},{32,104},{40,112},{48,120},{56,128},... | collective-permute-start | bytes 1179656 | tf_op jit(solution)/shard_map/ppermute | solution.py:15
  419.1 23.5 %collective-permute-start.10 = (f32[2,3,128,128]{3,2,1,0:T(8,128)S(1)}, f32[2,3,128,128]{3,2,1,0:T(8,128)}, u32[]{:S(2)}, u32[]{:S(2)}) collective-permute-start(f32[2,3,128,128]{3,2,1,0:T(8,128)S(1)} %get-tuple-element.124), channel_id=1, source_target_pairs={{0,8},{8,16},{16,24},{24,32},{32,40},{40,48},{48,56},{56,64},{64,7... | collective-permute-start | bytes 1179656 | tf_op jit(solution)/shard_map/ppermute | solution.py:15
  424.3 241.7 %copy-start.2 = (f32[2,3,128,128]{3,2,1,0:T(8,128)S(1)}, f32[2,3,128,128]{3,2,1,0:T(8,128)}, u32[]{:S(2)}) copy-start(f32[2,3,128,128]{3,2,1,0:T(8,128)} %get-tuple-element.120) | copy-start | bytes 1179652
  424.3 241.7 %all-reduce.27.cloned.1.call-start = ((), (), s32[]{:S(2)}) async-start(), calls=%async_computation.2 | async-start | bytes 1310720 | tf_op jit(solution)/shard_map/psum | solution.py:125
  666.0 1.1 copy-start.3
Sparse Core Ops, SparseCore 0:
  103.6 162.8 all-reduce.22
  269.2 68.9 all-reduce.28
  424.4 170.1 all-reduce.24
  597.0 68.9 all-reduce.26
